TPU v7x, 32 devices: a whole 2x2x4 slice. The times are simulated.
32 devices in a mesh: fsdp: 8 (over z, x), context: 4 (over y, core).
Axes of the slice: x: 2, y: 2, z: 4, core: 2. Of those that a mesh axis runs over, the one named last changes fastest.
Arguments:
- tokens: bfloat16 [16, 1024, 1536], P('fsdp', 'context'), may hold values from -6 to 6
- segments: int32 [16, 1024], P('fsdp', 'context'), may hold values from 0 to 15, never falling along the last dimension, each value on 1 to 512 neighbouring positions
- w_query: bfloat16 [1536, 1536], P('fsdp'), may hold values from -0.15625 to 0.15625
- w_key: bfloat16 [1536, 768], P('fsdp'), may hold values from -0.15625 to 0.15625
- w_value: bfloat16 [1536, 768], P('fsdp'), may hold values from -0.15625 to 0.15625
- w_out: bfloat16 [1536, 1536], P('fsdp'), may hold values from -0.875 to 0.875
- w_gate: bfloat16 [1536, 4096], P('fsdp', 'context'), may hold values from -0.15625 to 0.15625
- w_up: bfloat16 [1536, 4096], P('fsdp', 'context'), may hold values from -0.15625 to 0.15625
- w_down: bfloat16 [4096, 1536], P('context', 'fsdp'), may hold values from -0.09375 to 0.09375
- gain_attn: bfloat16 [1536], P('fsdp'), may hold values from 0.5 to 1.5
- gain_mlp: bfloat16 [1536], P('fsdp'), may hold values from 0.5 to 1.5
- cotangent: bfloat16 [16, 1024, 1536], P('fsdp', 'context'), may hold values from -6 to 6
Outputs:
- output: bfloat16 [16, 1024, 1536], P('fsdp', 'context')
- grad_tokens: float32 [16, 1024, 1536], P('fsdp', 'context')
- grad_w_query: float32 [1536, 1536], P('fsdp')
- grad_w_key: float32 [1536, 768], P('fsdp')
- grad_w_value: float32 [1536, 768], P('fsdp')
- grad_w_out: float32 [1536, 1536], P('fsdp')
- grad_w_gate: float32 [1536, 4096], P('fsdp', 'context')
- grad_w_up: float32 [1536, 4096], P('fsdp', 'context')
- grad_w_down: float32 [4096, 1536], P('context', 'fsdp')
- grad_gain_attn: float32 [1536], P('fsdp')
- grad_gain_mlp: float32 [1536], P('fsdp')
Inputs may be any that keep to these rules, and one draw needn't show every extreme that they name: `segments`: in each sequence segment numbers never fall and all 16 documents appear; the longest has exactly 512 tokens.
All inputs are finite; a program needn't handle non-finite values.
Results may differ from a plain program's by a relative error of at most 0.02.
Values may be sent and summed in bfloat16 or wider, within the bound.
No kernel may reach another device: no remote copies, remote signals or barrier semaphores. Data moves between devices by JAX's collectives and lax.ppermute only.
A program may use at most 256 MiB of HBM per device.

v0:
```python
import math
import jax
import jax.numpy as jnp
from jax import lax
from jax.sharding import PartitionSpec as P

H = 16
KVH = 8
HD = 96
EPSILON = 1e-05
THETA = 100000.0


def rms_scale(values, gain):
    return values * lax.rsqrt(jnp.mean(values * values, axis=-1, keepdims=True) + EPSILON) * gain


def rotate(values, cosines, sines):
    half_width = values.shape[-1] // 2
    leading = values[..., :half_width]
    trailing = values[..., half_width:]
    return jnp.concatenate(
        [leading * cosines - trailing * sines, trailing * cosines + leading * sines], axis=-1
    )


def gated(gate_act, up_act):
    return jax.nn.silu(gate_act) * up_act


def inner(left, right):
    return jnp.einsum("ti,tj->ij", left, right, preferred_element_type=jnp.float32)


def outer_back(grad_rows, weight):
    return jnp.einsum("ti,ji->tj", grad_rows, weight, preferred_element_type=jnp.float32)


def reduce_grads(parts):
    shares = (
        lax.psum_scatter(
            parts[0].astype(jnp.bfloat16), "fsdp", scatter_dimension=0, tiled=True
        ).astype(jnp.float32),
        lax.psum_scatter(
            parts[1].astype(jnp.bfloat16), "fsdp", scatter_dimension=0, tiled=True
        ).astype(jnp.float32),
        lax.psum_scatter(
            parts[2].astype(jnp.bfloat16), "fsdp", scatter_dimension=0, tiled=True
        ).astype(jnp.float32),
        lax.psum_scatter(
            parts[3].astype(jnp.bfloat16), "fsdp", scatter_dimension=0, tiled=True
        ).astype(jnp.float32),
        lax.psum_scatter(
            parts[4].astype(jnp.bfloat16), "fsdp", scatter_dimension=0, tiled=True
        ).astype(jnp.float32),
        lax.psum_scatter(
            parts[5].astype(jnp.bfloat16), "fsdp", scatter_dimension=0, tiled=True
        ).astype(jnp.float32),
    )
    result = (
        lax.psum(shares[0].astype(jnp.bfloat16), "context").astype(jnp.float32),
        lax.psum(shares[1].astype(jnp.bfloat16), "context").astype(jnp.float32),
        lax.psum(shares[2].astype(jnp.bfloat16), "context").astype(jnp.float32),
        lax.psum(shares[3].astype(jnp.bfloat16), "context").astype(jnp.float32),
        lax.psum(shares[4].astype(jnp.bfloat16), "context").astype(jnp.float32),
        lax.psum(shares[5].astype(jnp.bfloat16), "context").astype(jnp.float32),
    )
    return result


def gather_attention(shard_query, shard_key, shard_value, shard_out, shard_gain_a, shard_gain_m):
    return (
        lax.all_gather(shard_query, "fsdp", axis=0, tiled=True),
        lax.all_gather(shard_key, "fsdp", axis=0, tiled=True),
        lax.all_gather(shard_value, "fsdp", axis=0, tiled=True),
        lax.all_gather(shard_out, "fsdp", axis=0, tiled=True),
        lax.all_gather(shard_gain_a, "fsdp", axis=0, tiled=True),
        lax.all_gather(shard_gain_m, "fsdp", axis=0, tiled=True),
    )


def gather_mlp(shard_gate, shard_up, shard_down):
    return (
        lax.all_gather(shard_gate, "fsdp", axis=0, tiled=True),
        lax.all_gather(shard_up, "fsdp", axis=0, tiled=True),
        lax.all_gather(shard_down, "fsdp", axis=1, tiled=True),
    )


def on_device(
    tokens,
    segments,
    w_query,
    w_key,
    w_value,
    w_out,
    w_gate,
    w_up,
    w_down,
    gain_attn,
    gain_mlp,
    cotangent,
):
    seq_count, tok_local, model_width = tokens.shape
    row_count = seq_count * tok_local
    groups = H // KVH
    kv_width = KVH * HD
    logit_scale = 1.0 / math.sqrt(HD)
    whole_seg = lax.all_gather(segments, "context", axis=1, tiled=True)
    length = whole_seg.shape[1]
    all_rows = seq_count * length
    offset = lax.axis_index("context") * tok_local
    key_index = jnp.arange(length, dtype=jnp.int32)
    query_index = offset + jnp.arange(tok_local, dtype=jnp.int32)
    starts = jnp.concatenate(
        [jnp.ones((seq_count, 1), dtype=bool), whole_seg[:, 1:] != whole_seg[:, :-1]], axis=1
    )
    first_index = lax.cummax(jnp.where(starts, key_index[None, :], 0), axis=1)
    positions = lax.dynamic_slice_in_dim(key_index[None, :] - first_index, offset, tok_local, 1)
    frequency = jnp.power(THETA, -(jnp.arange(HD // 2, dtype=jnp.float32) * 2.0 / HD))
    angles = positions.astype(jnp.float32)[:, :, None] * frequency[None, None, :]
    cosines = jnp.cos(angles).reshape(row_count, 1, HD // 2)
    sines = jnp.sin(angles).reshape(row_count, 1, HD // 2)
    x_flat = tokens.reshape(row_count, model_width).astype(jnp.float32)

    def masked_scores(query_sequence, k_seq, q_seg, k_seg):
        unscaled_scores = (
            jnp.einsum(
                "wxif,axf->xiwa",
                query_sequence,
                k_seq.reshape(length, KVH, HD),
                preferred_element_type=jnp.float32,
            )
            * logit_scale
        )
        allowed = (q_seg[:, None] == k_seg[None, :]) & (key_index[None, :] <= query_index[:, None])
        return jnp.where(allowed[None, None], unscaled_scores, -1e30)

    def attend(items):
        query_sequence, k_seq, v_seq, q_seg, k_seg = items
        scores = masked_scores(query_sequence, k_seq, q_seg, k_seg)
        top_score = jnp.max(scores, axis=-1, keepdims=True)
        weights = jnp.exp(scores - top_score)
        total = jnp.sum(weights, axis=-1, keepdims=True)
        attention_probabilities = (weights / total).astype(jnp.bfloat16)
        mixed_seq = jnp.einsum(
            "uvqe,eua->quva",
            attention_probabilities,
            v_seq.reshape(length, KVH, HD),
            preferred_element_type=jnp.float32,
        ).astype(jnp.bfloat16)
        return (mixed_seq, top_score + jnp.log(total))

    def forward(attn_weights, mlp_weights):
        full_query, full_key, full_value, full_out, full_gain_a, full_gain_m = attn_weights
        normed = rms_scale(x_flat, full_gain_a.astype(jnp.float32)).astype(jnp.bfloat16)
        queries = jnp.dot(normed, full_query, preferred_element_type=jnp.float32).reshape(
            row_count, H, HD
        )
        key_rows = jnp.dot(normed, full_key, preferred_element_type=jnp.float32).reshape(
            row_count, KVH, HD
        )
        value_matrix_rows = jnp.dot(normed, full_value, preferred_element_type=jnp.float32).astype(
            jnp.bfloat16
        )
        qrot = (
            rotate(queries, cosines, sines)
            .astype(jnp.bfloat16)
            .reshape(seq_count, tok_local, KVH, groups, HD)
        )
        rotary_keys = (
            rotate(key_rows, cosines, sines)
            .astype(jnp.bfloat16)
            .reshape(seq_count, tok_local, kv_width)
        )
        all_keys, all_values = (
            lax.all_gather(rotary_keys, "context", axis=1, tiled=True),
            lax.all_gather(
                value_matrix_rows.reshape(seq_count, tok_local, kv_width),
                "context",
                axis=1,
                tiled=True,
            ),
        )
        mixed, log_totals = lax.map(attend, (qrot, all_keys, all_values, segments, whole_seg))
        mixed_flat = mixed.reshape(row_count, H * HD)
        resid = x_flat + jnp.dot(mixed_flat, full_out, preferred_element_type=jnp.float32)
        full_gate, full_up, full_down = mlp_weights
        normed_two = rms_scale(resid, full_gain_m.astype(jnp.float32)).astype(jnp.bfloat16)
        all_normed_two = lax.all_gather(
            normed_two.reshape(seq_count, tok_local, model_width), "context", axis=1, tiled=True
        ).reshape(all_rows, model_width)
        gate_act = jnp.dot(all_normed_two, full_gate, preferred_element_type=jnp.float32)
        up_act = jnp.dot(all_normed_two, full_up, preferred_element_type=jnp.float32)
        hidden = gated(gate_act, up_act).astype(jnp.bfloat16)
        partial_down = jnp.dot(hidden, full_down, preferred_element_type=jnp.float32)
        down_sum = (
            lax.psum_scatter(
                partial_down.reshape(seq_count, length, model_width).astype(jnp.bfloat16),
                "context",
                scatter_dimension=1,
                tiled=True,
            )
            .astype(jnp.float32)
            .reshape(row_count, model_width)
        )
        final = resid + down_sum
        return (
            final,
            normed,
            qrot,
            all_keys,
            all_values,
            mixed,
            log_totals,
            resid,
            all_normed_two,
            gate_act,
            up_act,
            hidden,
        )

    attn_weights = gather_attention(w_query, w_key, w_value, w_out, gain_attn, gain_mlp)
    mlp_weights = gather_mlp(w_gate, w_up, w_down)
    state = forward(attn_weights, mlp_weights)
    output = state[0].astype(jnp.bfloat16).reshape(seq_count, tok_local, model_width)
    fresh = lax.optimization_barrier(
        (w_query, w_key, w_value, w_out, gain_attn, gain_mlp, w_gate, w_up, w_down, output)
    )
    attn_weights = gather_attention(fresh[0], fresh[1], fresh[2], fresh[3], fresh[4], fresh[5])
    mlp_weights = gather_mlp(fresh[6], fresh[7], fresh[8])
    state = forward(attn_weights, mlp_weights)
    (
        final,
        normed,
        qrot,
        all_keys,
        all_values,
        mixed,
        log_totals,
        resid,
        all_normed_two,
        gate_act,
        up_act,
        hidden,
    ) = state
    full_query, full_key, full_value, full_out, full_gain_a, full_gain_m = attn_weights
    full_gate, full_up, full_down = mlp_weights
    grad_out = cotangent.reshape(row_count, model_width)
    all_grad_out = lax.all_gather(cotangent, "context", axis=1, tiled=True).reshape(
        all_rows, model_width
    )
    grad_down_t = inner(all_grad_out, hidden)
    grad_hidden = outer_back(all_grad_out, full_down)
    gate_pull = jax.vjp(gated, gate_act, up_act)[1]
    grad_gate_f, grad_up_f = gate_pull(grad_hidden)
    grad_gate_act = grad_gate_f.astype(jnp.bfloat16)
    grad_up_act = grad_up_f.astype(jnp.bfloat16)
    grad_gate = inner(all_normed_two, grad_gate_act)
    grad_up = inner(all_normed_two, grad_up_act)
    part_normed_two = outer_back(grad_gate_act, full_gate) + outer_back(grad_up_act, full_up)
    grad_normed_two = lax.psum_scatter(
        part_normed_two.reshape(seq_count, length, model_width),
        "context",
        scatter_dimension=1,
        tiled=True,
    ).reshape(row_count, model_width)
    norm_pull = jax.vjp(rms_scale, resid, full_gain_m.astype(jnp.float32))[1]
    back_resid, grad_gain_m = norm_pull(grad_normed_two)
    mlp_shares = (
        lax.psum_scatter(
            grad_gate.astype(jnp.bfloat16), "fsdp", scatter_dimension=0, tiled=True
        ).astype(jnp.float32),
        lax.psum_scatter(
            grad_up.astype(jnp.bfloat16), "fsdp", scatter_dimension=0, tiled=True
        ).astype(jnp.float32),
        lax.psum_scatter(
            grad_down_t.astype(jnp.bfloat16), "fsdp", scatter_dimension=0, tiled=True
        ).astype(jnp.float32),
    )
    grad_resid = grad_out.astype(jnp.float32) + back_resid
    grad_attn = grad_resid.astype(jnp.bfloat16)
    mixed_flat = mixed.reshape(row_count, H * HD)
    grad_out_w = inner(mixed_flat, grad_attn)
    grad_mixed = (
        outer_back(grad_attn, full_out)
        .astype(jnp.bfloat16)
        .reshape(seq_count, tok_local, KVH, groups, HD)
    )

    def attend_back(items):
        query_sequence, k_seq, v_seq, q_seg, k_seg, log_total, grad_seq = items
        scores = masked_scores(query_sequence, k_seq, q_seg, k_seg)
        attention_probabilities = jnp.exp(scores - log_total)
        grad_probs = jnp.einsum(
            "wxif,axf->xiwa",
            grad_seq,
            v_seq.reshape(length, KVH, HD),
            preferred_element_type=jnp.float32,
        )
        weighted = jnp.sum(attention_probabilities * grad_probs, axis=-1, keepdims=True)
        score_gradient = (attention_probabilities * (grad_probs - weighted)).astype(jnp.bfloat16)
        grad_q = (
            jnp.einsum(
                "uvqe,eua->quva",
                score_gradient,
                k_seq.reshape(length, KVH, HD),
                preferred_element_type=jnp.float32,
            )
            * logit_scale
        )
        grad_k = (
            jnp.einsum(
                "jnbp,bjny->pjy", score_gradient, query_sequence, preferred_element_type=jnp.float32
            )
            * logit_scale
        )
        grad_v = jnp.einsum(
            "jnbp,bjny->pjy",
            attention_probabilities.astype(jnp.bfloat16),
            grad_seq,
            preferred_element_type=jnp.float32,
        )
        return (grad_q, grad_k.reshape(length, kv_width), grad_v.reshape(length, kv_width))

    grad_qrot, part_keys, part_values = lax.map(
        attend_back, (qrot, all_keys, all_values, segments, whole_seg, log_totals, grad_mixed)
    )
    grad_krot, grad_vals = (
        lax.psum_scatter(
            part_keys.astype(jnp.bfloat16), "context", scatter_dimension=1, tiled=True
        ).astype(jnp.float32),
        lax.psum_scatter(
            part_values.astype(jnp.bfloat16), "context", scatter_dimension=1, tiled=True
        ).astype(jnp.float32),
    )
    grad_queries = (
        rotate(grad_qrot.reshape(row_count, H, HD), cosines, -sines)
        .astype(jnp.bfloat16)
        .reshape(row_count, H * HD)
    )
    grad_keys = (
        rotate(grad_krot.reshape(row_count, KVH, HD), cosines, -sines)
        .astype(jnp.bfloat16)
        .reshape(row_count, kv_width)
    )
    grad_values = grad_vals.reshape(row_count, kv_width).astype(jnp.bfloat16)
    grad_query_w = inner(normed, grad_queries)
    grad_key_w = inner(normed, grad_keys)
    grad_value_w = inner(normed, grad_values)
    grad_normed = (
        outer_back(grad_queries, full_query)
        + outer_back(grad_keys, full_key)
        + outer_back(grad_values, full_value)
    )
    first_pull = jax.vjp(rms_scale, x_flat, full_gain_a.astype(jnp.float32))[1]
    back_input, grad_gain_a = first_pull(grad_normed)
    attn_grads = reduce_grads(
        (grad_query_w, grad_key_w, grad_value_w, grad_out_w, grad_gain_a, grad_gain_m)
    )
    grad_input = (grad_resid + back_input).reshape(seq_count, tok_local, model_width)
    return (
        output,
        grad_input,
        attn_grads[0],
        attn_grads[1],
        attn_grads[2],
        attn_grads[3],
        mlp_shares[0],
        mlp_shares[1],
        jnp.transpose(mlp_shares[2]),
        attn_grads[4],
        attn_grads[5],
    )


def solution(mesh):
    return jax.shard_map(
        on_device,
        mesh=mesh,
        in_specs=(
            P("fsdp", "context", None),
            P("fsdp", "context"),
            P("fsdp", None),
            P("fsdp", None),
            P("fsdp", None),
            P("fsdp", None),
            P("fsdp", "context"),
            P("fsdp", "context"),
            P("context", "fsdp"),
            P("fsdp"),
            P("fsdp"),
            P("fsdp", "context", None),
        ),
        out_specs=(
            P("fsdp", "context", None),
            P("fsdp", "context", None),
            P("fsdp", None),
            P("fsdp", None),
            P("fsdp", None),
            P("fsdp", None),
            P("fsdp", "context"),
            P("fsdp", "context"),
            P("context", "fsdp"),
            P("fsdp"),
            P("fsdp"),
        ),
        check_vma=False,
    )
```

profile of v0, /device:TPU:0, one launch (start us, length us, event | category | flops | bytes accessed | tf_op | source)
XLA Modules:
  0.0 2307.0 jit_solution(10528098979458675509)
XLA Ops:
  13.2 23.4 %all-reduce.9 = (bf16[1536]{0:T(1024)(128)(2,1)S(1)}, bf16[1536]{0:T(1024)(128)(2,1)S(1)}) all-reduce(bf16[1536]{0:T(1024)(128)(2,1)S(1)} %dynamic-update-slice, bf16[1536]{0:T(1024)(128)(2,1)S(1)} %dynamic-update-slice.1), channel_id=1, replica_groups=mesh['fsdp'=8,'context'=4] {'fsdp'}, use_global_device_ids=true, to_apply=%add.1 | all-reduce | flops 3072 | bytes 12288
  47.7 17.6 all-gather.26.cloned.1.call-done
  75.2 43.1 %all-gather.22.cloned.1.call-done = bf16[1536,768]{1,0:T(8,128)(2,1)} async-done(((bf16[192,768]{1,0:T(8,128)(2,1)}), bf16[1536,768]{1,0:T(8,128)(2,1)}) %all-gather.22.cloned.1.call-update) | async-done | bytes 2359312 | tf_op jit(solution)/shard_map/all_gather | solution.py:75
  124.8 74.1 %all-gather.30.cloned.1.call-done = bf16[1536,1536]{1,0:T(8,128)(2,1)} async-done(((bf16[192,1536]{1,0:T(8,128)(2,1)}), bf16[1536,1536]{1,0:T(8,128)(2,1)}) %all-gather.30.cloned.1.call-update) | async-done | bytes 4718608 | tf_op jit(solution)/shard_map/all_gather | solution.py:73
  213.0 15.0 all-gather.28.cloned.1.call-done
  228.0 30.9 %all-gather.24.cloned.1.call-done = bf16[2,1024,768]{1,2,0:T(8,128)(2,1)} async-done(((bf16[2,256,768]{1,2,0:T(8,128)(2,1)}), bf16[2,1024,768]{1,2,0:T(8,128)(2,1)}) %all-gather.24.cloned.1.call-update) | async-done | bytes 3145744 | tf_op jit(solution)/shard_map/all_gather | solution.py:178
  260.3 43.3 %while.39 = (s32[]{:T(128)}, bf16[2,256,8,2,96]{1,4,3,2,0:T(8,128)(2,1)}, bf16[2,1024,768]{1,2,0:T(8,128)(2,1)}, s32[2,256]{1,0:T(2,128)S(1)}, s32[2,1024]{1,0:T...) while((s32[]{:T(128)}, ...), condition=%wide.region_6.7_spmd.clone, body=%wide.region_3.6_spmd.clone.sunk | while | flops 1636959488 | bytes 45139068 | solution.py:185
  262.7 10.7 fusion.224
  273.5 8.2 fusion.225
  284.1 10.7 fusion.224
  294.9 8.7 fusion.225
  307.1 33.8 %all-gather.32.cloned.1.call-done = bf16[1536,1536]{1,0:T(8,128)(2,1)} async-done(((bf16[192,1536]{1,0:T(8,128)(2,1)}), bf16[1536,1536]{1,0:T(8,128)(2,1)}) %all-gather.32.cloned.1.call-update) | async-done | bytes 4718608 | tf_op jit(solution)/shard_map/all_gather | solution.py:76
  350.8 50.9 %all-gather.36.cloned.1.call-done = bf16[1536,1024]{1,0:T(8,128)(2,1)} async-done(((bf16[192,1024]{1,0:T(8,128)(2,1)}), bf16[1536,1024]{1,0:T(8,128)(2,1)}) %all-gather.36.cloned.1.call-update) | async-done | bytes 3145744 | tf_op jit(solution)/shard_map/all_gather | solution.py:84
  401.7 47.2 %all-gather.34.cloned.1.call-done = bf16[2,1024,1536]{2,1,0:T(8,128)(2,1)} async-done(((bf16[2,256,1536]{2,1,0:T(8,128)(2,1)}), bf16[2,1024,1536]{2,1,0:T(8,128)(2,1)}) %all-gather.34.cloned.1.call-update) | async-done | bytes 6291472 | tf_op jit(solution)/shard_map/all_gather | solution.py:190
  448.9 11.7 fusion.118
  460.6 51.0 %all-gather.38.cloned.1.call-done = bf16[1536,1024]{1,0:T(8,128)(2,1)} async-done(((bf16[192,1024]{1,0:T(8,128)(2,1)}), bf16[1536,1024]{1,0:T(8,128)(2,1)}) %all-gather.38.cloned.1.call-update) | async-done | bytes 3145744 | tf_op jit(solution)/shard_map/all_gather | solution.py:85
  511.5 61.1 %all-gather.40.cloned.1.call-done = bf16[1024,1536]{0,1:T(8,128)(2,1)} async-done(((bf16[1024,192]{0,1:T(8,128)(2,1)}), bf16[1024,1536]{0,1:T(8,128)(2,1)}) %all-gather.40.cloned.1.call-update) | async-done | bytes 3145744 | tf_op jit(solution)/shard_map/all_gather | solution.py:86
  572.7 20.2 convolution_convert_fusion.2
  593.0 57.1 %reduce-scatter.14.cloned.1.call-done = bf16[2,256,1536]{2,1,0:T(8,128)(2,1)} async-done(((bf16[2,1024,1536]{2,1,0:T(8,128)(2,1)}), bf16[2,256,1536]{2,1,0:T(8,128)(2,1)}) %reduce-scatter.14.cloned.1.call-update) | async-done | bytes 1572880 | tf_op jit(solution)/shard_map/reduce_scatter | solution.py:198
  655.9 21.6 all-reduce.8
  678.0 28.5 %all-gather.46.cloned.1.call-done = bf16[1536,768]{1,0:T(8,128)(2,1)} async-done(((bf16[192,768]{1,0:T(8,128)(2,1)}), bf16[1536,768]{1,0:T(8,128)(2,1)}) %all-gather.46.cloned.1.call-update) | async-done | bytes 2359312 | tf_op jit(solution)/shard_map/all_gather | solution.py:75
  713.2 46.3 %all-gather.50.cloned.1.call-done = bf16[1536,768]{1,0:T(8,128)(2,1)} async-done(((bf16[192,768]{1,0:T(8,128)(2,1)}), bf16[1536,768]{1,0:T(8,128)(2,1)}) %all-gather.50.cloned.1.call-update) | async-done | bytes 2359312 | tf_op jit(solution)/shard_map/all_gather | solution.py:74
  770.0 70.3 %all-gather.54.cloned.1.call-done = bf16[1536,1536]{1,0:T(8,128)(2,1)} async-done(((bf16[192,1536]{1,0:T(8,128)(2,1)}), bf16[1536,1536]{1,0:T(8,128)(2,1)}) %all-gather.54.cloned.1.call-update) | async-done | bytes 4718608 | tf_op jit(solution)/shard_map/all_gather | solution.py:73
  852.9 16.5 all-gather.48.cloned.1.call-done
  869.4 31.0 %all-gather.52.cloned.1.call-done = bf16[2,1024,768]{1,2,0:T(8,128)(2,1)} async-done(((bf16[2,256,768]{1,2,0:T(8,128)(2,1)}), bf16[2,1024,768]{1,2,0:T(8,128)(2,1)}) %all-gather.52.cloned.1.call-update) | async-done | bytes 3145744 | tf_op jit(solution)/shard_map/all_gather | solution.py:177
  901.8 57.2 %while.40 = (s32[]{:T(128)}, bf16[2,256,8,2,96]{1,4,3,2,0:T(8,128)(2,1)}, f32[2,8,2,256,1]{3,2,1,4,0:T(2,128)S(1)}, bf16[2,1024,768]{1,2,0:T(8,128)(2,1)}, s32[2...) while((s32[]{:T(128)}, ...), condition=%wide.region_12.13_spmd.clone, body=%wide.region_9.12_spmd.clone.sunk | while | flops 1662120192 | bytes 62538888 | solution.py:185
  911.9 9.2 fusion.230
  921.1 9.1 fusion.231
  940.4 9.2 fusion.230
  949.6 9.1 fusion.231
  963.7 19.0 all-gather.56.cloned.1.call-done
  993.2 50.3 %all-gather.62.cloned.1.call-done = bf16[1536,1024]{1,0:T(8,128)(2,1)} async-done(((bf16[192,1024]{1,0:T(8,128)(2,1)}), bf16[1536,1024]{1,0:T(8,128)(2,1)}) %all-gather.62.cloned.1.call-update) | async-done | bytes 3145744 | tf_op jit(solution)/shard_map/all_gather | solution.py:84
  1043.5 46.7 %all-gather.58.cloned.1.call-done = bf16[2,1024,1536]{2,1,0:T(8,128)(2,1)} async-done(((bf16[2,256,1536]{2,1,0:T(8,128)(2,1)}), bf16[2,1024,1536]{2,1,0:T(8,128)(2,1)}) %all-gather.58.cloned.1.call-update) | async-done | bytes 6291472 | tf_op jit(solution)/shard_map/all_gather | solution.py:190
  1090.2 11.7 fusion.122
  1101.9 51.0 %all-gather.60.cloned.1.call-done = bf16[1536,1024]{1,0:T(8,128)(2,1)} async-done(((bf16[192,1024]{1,0:T(8,128)(2,1)}), bf16[1536,1024]{1,0:T(8,128)(2,1)}) %all-gather.60.cloned.1.call-update) | async-done | bytes 3145744 | tf_op jit(solution)/shard_map/all_gather | solution.py:85
  1153.0 11.7 fusion.121
  1164.6 35.0 %all-gather.44.cloned.1.call-done = bf16[2,1024,1536]{2,1,0:T(8,128)(2,1)} async-done(((bf16[2,256,1536]{2,1,0:T(8,128)(2,1)}), bf16[2,1024,1536]{2,1,0:T(8,128)(2,1)}) %all-gather.44.cloned.1.call-update) | async-done | bytes 6291472 | tf_op jit(solution)/shard_map/all_gather | solution.py:250
  1199.6 62.9 %all-gather.42.cloned.1.call-done = bf16[1024,1536]{0,1:T(8,128)(2,1)} async-done(((bf16[1024,192]{0,1:T(8,128)(2,1)}), bf16[1024,1536]{0,1:T(8,128)(2,1)}) %all-gather.42.cloned.1.call-update) | async-done | bytes 3145744 | tf_op jit(solution)/shard_map/all_gather | solution.py:86
  1262.5 16.1 fusion.78
  1278.6 9.4 fusion.123
  1288.0 13.0 convolution_add_fusion
  1301.2 97.8 %reduce-scatter.16.cloned.1.call-done = f32[2,256,1536]{2,1,0:T(8,128)} async-done(((f32[2,1024,1536]{2,1,0:T(8,128)}), f32[2,256,1536]{2,1,0:T(8,128)}) %reduce-scatter.16.cloned.1.call-update) | async-done | bytes 3145744 | tf_op jit(solution)/shard_map/reduce_scatter | solution.py:262
  1417.6 172.9 %while.41 = (s32[]{:T(128)}, f32[2,256,8,2,96]{1,0,4,3,2:T(2,128)}, bf16[2,1024,768]{1,2,0:T(8,128)(2,1)}, bf16[2,1024,768]{2,1,0:T(8,128)(2,1)}, bf16[2,1024,76...) while((s32[]{:T(128)}, f32[2,256,8,2,96]{1,0,4,3,2:T(2,128)}, ...), condition=%wide.region_18.19_spmd.clone, body=%wide.region_16.18_spmd.clone.sunk | while | flops 4067029248 | bytes 192513344 | solution.py:326
  1424.2 10.7 fusion.243
  1434.9 9.9 fusion.244
  1444.8 8.7 fusion.245
  1467.8 32.3 %dynamic_update_slice.44 = f32[2,256,8,2,96]{1,0,4,3,2:T(2,128)} dynamic-update-slice(f32[2,256,8,2,96]{1,0,4,3,2:T(2,128)} %get-tuple-element.728, f32[1,256,8,2,96]{1,0,4,3,2:T(1,128)S(1)} %copy.145, s32[]{:T(128)S(6)} %copy.177, s32[]{:T(128)} %constant.103.clone.1..sunk, s32[]{:T(128)} %constant.103.clone.1..sunk, s32[]{:T(128)} %constant.103.clone.1..sunk, s32[]{:T(128)} %constant.103.clone.1..sunk) | dynamic-update-slice | bytes 3145732 | tf_op jit(solution)/shard_map/while/body/jit(dynamic_update_index_in_dim)/dynamic_update_slice | solution.py:326
  1510.5 10.7 fusion.243
  1521.2 9.9 fusion.244
  1531.0 8.7 fusion.245
  1554.1 32.3 %dynamic_update_slice.44 = f32[2,256,8,2,96]{1,0,4,3,2:T(2,128)} dynamic-update-slice(f32[2,256,8,2,96]{1,0,4,3,2:T(2,128)} %get-tuple-element.728, f32[1,256,8,2,96]{1,0,4,3,2:T(1,128)S(1)} %copy.145, s32[]{:T(128)S(6)} %copy.177, s32[]{:T(128)} %constant.103.clone.1..sunk, s32[]{:T(128)} %constant.103.clone.1..sunk, s32[]{:T(128)} %constant.103.clone.1..sunk, s32[]{:T(128)} %constant.103.clone.1..sunk) | dynamic-update-slice | bytes 3145732 | tf_op jit(solution)/shard_map/while/body/jit(dynamic_update_index_in_dim)/dynamic_update_slice | solution.py:326
  1591.3 15.8 fusion.82
  1610.2 11.3 convolution_convert_fusion.3
  1621.5 11.4 convolution_convert_fusion.4
  1659.1 10.1 reduce-scatter.20.cloned.1.call-done
  1673.8 73.5 %reduce-scatter.34.cloned.1.call-done = bf16[192,1024]{1,0:T(8,128)(2,1)} async-done(((bf16[1536,1024]{1,0:T(8,128)(2,1)}), bf16[192,1024]{1,0:T(8,128)(2,1)}) %reduce-scatter.34.cloned.1.call-update) | async-done | bytes 393232
  1749.8 74.8 %reduce-scatter.32.cloned.1.call-done = bf16[192,1024]{1,0:T(8,128)(2,1)} async-done(((bf16[1536,1024]{1,0:T(8,128)(2,1)}), bf16[192,1024]{1,0:T(8,128)(2,1)}) %reduce-scatter.32.cloned.1.call-update) | async-done | bytes 393232 | tf_op jit(solution)/shard_map/reduce_scatter | solution.py:274
  1826.5 75.5 %reduce-scatter.30.cloned.1.call-done = bf16[192,1024]{1,0:T(8,128)(2,1)} async-done(((bf16[1536,1024]{1,0:T(8,128)(2,1)}), bf16[192,1024]{1,0:T(8,128)(2,1)}) %reduce-scatter.30.cloned.1.call-update) | async-done | bytes 393232 | tf_op jit(solution)/shard_map/reduce_scatter | solution.py:271
  1915.2 85.3 %reduce-scatter.28.cloned.1.call-done = bf16[192,1536]{1,0:T(8,128)(2,1)} async-done(((bf16[1536,1536]{1,0:T(8,128)(2,1)}), bf16[192,1536]{1,0:T(8,128)(2,1)}) %reduce-scatter.28.cloned.1.call-update) | async-done | bytes 589840 | tf_op jit(solution)/shard_map/reduce_scatter | solution.py:50
  2000.5 99.1 %reduce-scatter.22.cloned.1.call-done = bf16[192,1536]{1,0:T(8,128)(2,1)} async-done(((bf16[1536,1536]{1,0:T(8,128)(2,1)}), bf16[192,1536]{1,0:T(8,128)(2,1)}) %reduce-scatter.22.cloned.1.call-update) | async-done | bytes 589840 | tf_op jit(solution)/shard_map/reduce_scatter | solution.py:41
  2099.7 72.7 %reduce-scatter.24.cloned.1.call-done = bf16[192,768]{1,0:T(8,128)(2,1)} async-done(((bf16[1536,768]{1,0:T(8,128)(2,1)}), bf16[192,768]{1,0:T(8,128)(2,1)}) %reduce-scatter.24.cloned.1.call-update) | async-done | bytes 294928 | tf_op jit(solution)/shard_map/reduce_scatter | solution.py:44
  2172.4 72.0 %reduce-scatter.26.cloned.1.call-done = bf16[192,768]{1,0:T(8,128)(2,1)} async-done(((bf16[1536,768]{1,0:T(8,128)(2,1)}), bf16[192,768]{1,0:T(8,128)(2,1)}) %reduce-scatter.26.cloned.1.call-update) | async-done | bytes 294928 | tf_op jit(solution)/shard_map/reduce_scatter | solution.py:47
  2244.5 19.4 all-reduce.7
  2276.2 16.7 all-reduce.14.cloned.1.call-done
  (353 shorter events, 277.5 us)
Async XLA Ops:
  7.2 38.9 %copy-start.5 = (bf16[2,256,1536]{2,1,0:T(8,128)(2,1)S(1)}, bf16[2,256,1536]{2,1,0:T(8,128)(2,1)}, u32[]{:S(2)}) copy-start(bf16[2,256,1536]{2,1,0:T(8,128)(2,1)} %param.18) | copy-start | bytes 4718596
  7.2 58.1 %all-gather.26.cloned.1.call-start = ((), (), s32[]{:S(2)}) async-start(), calls=%async_computation.13 | async-start | bytes 2654208 | tf_op jit(solution)/shard_map/all_gather | solution.py:74
  7.9 110.3 %all-gather.22.cloned.1.call-start = ((), (), s32[]{:S(2)}) async-start(), calls=%async_computation.11 | async-start | bytes 2654208 | tf_op jit(solution)/shard_map/all_gather | solution.py:75
  8.7 190.2 %all-gather.30.cloned.1.call-start = ((), (), s32[]{:S(2)}) async-start(), calls=%async_computation.15 | async-start | bytes 5308416 | tf_op jit(solution)/shard_map/all_gather | solution.py:73
  9.4 218.6 %all-gather.28.cloned.1.call-start = ((), (), s32[]{:S(2)}) async-start(), calls=%async_computation.14 | async-start | bytes 3932160 | tf_op jit(solution)/shard_map/all_gather | solution.py:177
  45.0 24.5 %copy-start.40 = (f32[2,256]{1,0:T(2,128)}, f32[2,256]{1,0:T(2,128)S(1)}, u32[]{:S(2)}) copy-start(f32[2,256]{1,0:T(2,128)S(1)} %get-tuple-element.446) | copy-start | bytes 6148
  46.1 164.4 %copy-start.17 = (f32[512,48]{0,1:T(8,128)}, f32[512,48]{0,1:T(8,128)S(1)}, u32[]{:S(2)}) copy-start(f32[512,48]{0,1:T(8,128)S(1)} %get-tuple-element.445) | copy-start | bytes 294916
  46.1 164.4 %copy-start.20 = (f32[512,48]{0,1:T(8,128)}, f32[512,48]{0,1:T(8,128)S(1)}, u32[]{:S(2)}) copy-start(f32[512,48]{0,1:T(8,128)S(1)} %get-tuple-element.444) | copy-start | bytes 294916
  74.6 184.3 %all-gather.24.cloned.1.call-start = ((), (), s32[]{:S(2)}) async-start(), calls=%async_computation.12 | async-start | bytes 3932160 | tf_op jit(solution)/shard_map/all_gather | solution.py:178
  74.7 46.6 %copy-start.38 = (f32[1,2,2,128]{3,1,2,0:T(2,128)}, f32[1,2,2,128]{3,1,2,0:T(2,128)S(1)}, u32[]{:S(2)}) copy-start(f32[1,2,2,128]{3,1,2,0:T(2,128)S(1)} %copy.131) | copy-start | bytes 6148
  74.7 46.6 %copy-start.35 = (f32[512]{0:T(512)}, f32[512]{0:T(512)S(1)}, u32[]{:S(2)}) copy-start(f32[512]{0:T(512)S(1)} %rsqrt.34) | copy-start | bytes 6148
  122.5 218.4 %all-gather.32.cloned.1.call-start = ((), (), s32[]{:S(2)}) async-start(), calls=%async_computation.16 | async-start | bytes 5308416 | tf_op jit(solution)/shard_map/all_gather | solution.py:76
  123.1 278.6 %all-gather.36.cloned.1.call-start = ((), (), s32[]{:S(2)}) async-start(), calls=%async_computation.18 | async-start | bytes 3538944 | tf_op jit(solution)/shard_map/all_gather | solution.py:84
  123.8 325.0 %all-gather.34.cloned.1.call-start = ((), (), s32[]{:S(2)}) async-start(), calls=%async_computation.17 | async-start | bytes 7864320 | tf_op jit(solution)/shard_map/all_gather | solution.py:190
  198.9 6.8 copy-start.27
  211.5 48.7 %copy-start.30 = (s32[2,256]{1,0:T(2,128)S(1)}, s32[2,256]{1,0:T(2,128)}, u32[]{:S(2)}) copy-start(s32[2,256]{1,0:T(2,128)} %param.19) | copy-start | bytes 6148
  303.6 37.3 %copy-start.6 = (bf16[2,256,1536]{2,1,0:T(8,128)(2,1)S(1)}, bf16[2,256,1536]{2,1,0:T(8,128)(2,1)}, u32[]{:S(2)}) copy-start(bf16[2,256,1536]{2,1,0:T(8,128)(2,1)} %param.18) | copy-start | bytes 4718596
  340.9 6.5 copy-start.34
  348.9 162.7 %all-gather.38.cloned.1.call-start = ((), (), s32[]{:S(2)}) async-start(), calls=%async_computation.19 | async-start | bytes 3538944 | tf_op jit(solution)/shard_map/all_gather | solution.py:85
  349.6 223.1 %all-gather.40.cloned.1.call-start = ((), (), s32[]{:S(2)}) async-start(), calls=%async_computation.20 | async-start | bytes 3538944 | tf_op jit(solution)/shard_map/all_gather | solution.py:86
  350.2 299.8 %reduce-scatter.14.cloned.1.call-start = ((), (), s32[]{:S(2)}) async-start(), calls=%async_computation.21 | async-start | bytes 7864320 | tf_op jit(solution)/shard_map/reduce_scatter | solution.py:198
  592.9 62.5 %copy-start.47 = (bf16[192]{0:T(256)(128)(2,1)S(1)}, bf16[192]{0:T(256)(128)(2,1)}, u32[]{:S(2)}) copy-start(bf16[192]{0:T(256)(128)(2,1)} %param.28) | copy-start | bytes 1156
  592.9 62.8 %copy-start.48 = (bf16[192]{0:T(256)(128)(2,1)S(1)}, bf16[192]{0:T(256)(128)(2,1)}, u32[]{:S(2)}) copy-start(bf16[192]{0:T(256)(128)(2,1)} %param.27) | copy-start | bytes 1156
  592.9 84.6 %copy-start.36 = (f32[512]{0:T(512)S(1)}, f32[512]{0:T(512)}, u32[]{:S(2)}) copy-start(f32[512]{0:T(512)} %copy-done.35) | copy-start | bytes 6148
  592.9 113.6 %all-gather.46.cloned.1.call-start = ((), (), s32[]{:S(2)}) async-start(), calls=%async_computation.24 | async-start | bytes 2654208 | tf_op jit(solution)/shard_map/all_gather | solution.py:75
  654.0 105.6 %all-gather.50.cloned.1.call-start = ((), (), s32[]{:S(2)}) async-start(), calls=%async_computation.26 | async-start | bytes 2654208 | tf_op jit(solution)/shard_map/all_gather | solution.py:74
  654.7 185.5 %all-gather.54.cloned.1.call-start = ((), (), s32[]{:S(2)}) async-start(), calls=%async_computation.28 | async-start | bytes 5308416 | tf_op jit(solution)/shard_map/all_gather | solution.py:73
  655.3 214.1 %all-gather.48.cloned.1.call-start = ((), (), s32[]{:S(2)}) async-start(), calls=%async_computation.25 | async-start | bytes 3932160 | tf_op jit(solution)/shard_map/all_gather | solution.py:178
  677.5 35.2 %copy-start.31 = (f32[1536]{0:T(1024)}, f32[1536]{0:T(1024)S(1)}, u32[]{:S(2)}) copy-start(f32[1536]{0:T(1024)S(1)} %convert_element_type.264) | copy-start | bytes 18436
  678.0 34.8 %copy-start.41 = (f32[2,256]{1,0:T(2,128)S(1)}, f32[2,256]{1,0:T(2,128)}, u32[]{:S(2)}) copy-start(f32[2,256]{1,0:T(2,128)} %copy-done.40) | copy-start | bytes 6148
  712.7 187.7 %all-gather.52.cloned.1.call-start = ((), (), s32[]{:S(2)}) async-start(), calls=%async_computation.27 | async-start | bytes 3932160 | tf_op jit(solution)/shard_map/all_gather | solution.py:177
  713.2 133.7 %copy-start.23 = (bf16[2,256,1536]{2,1,0:T(8,128)(2,1)}, bf16[2,256,1536]{2,1,0:T(8,128)(2,1)S(1)}, u32[]{:S(2)}) copy-start(bf16[2,256,1536]{2,1,0:T(8,128)(2,1)S(1)} %fusion.93) | copy-start | bytes 4718596
  768.5 214.1 %all-gather.56.cloned.1.call-start = ((), (), s32[]{:S(2)}) async-start(), calls=%async_computation.29 | async-start | bytes 5308416 | tf_op jit(solution)/shard_map/all_gather | solution.py:76
  769.1 274.4 %all-gather.62.cloned.1.call-start = ((), (), s32[]{:S(2)}) async-start(), calls=%async_computation.32 | async-start | bytes 3538944 | tf_op jit(solution)/shard_map/all_gather | solution.py:84
  769.8 320.4 %all-gather.58.cloned.1.call-start = ((), (), s32[]{:S(2)}) async-start(), calls=%async_computation.30 | async-start | bytes 7864320 | tf_op jit(solution)/shard_map/all_gather | solution.py:190
  959.0 23.7 %copy-start.7 = (bf16[2,256,1536]{2,1,0:T(8,128)(2,1)S(1)}, bf16[2,256,1536]{2,1,0:T(8,128)(2,1)}, u32[]{:S(2)}) copy-start(bf16[2,256,1536]{2,1,0:T(8,128)(2,1)} %param.18) | copy-start | bytes 4718596
  982.6 6.9 copy-start.33
  991.1 161.8 %all-gather.60.cloned.1.call-start = ((), (), s32[]{:S(2)}) async-start(), calls=%async_computation.31 | async-start | bytes 3538944 | tf_op jit(solution)/shard_map/all_gather | solution.py:85
  991.7 207.9 %all-gather.44.cloned.1.call-start = ((), (), s32[]{:S(2)}) async-start(), calls=%async_computation.23 | async-start | bytes 7864320 | tf_op jit(solution)/shard_map/all_gather | solution.py:250
  992.4 270.1 %all-gather.42.cloned.1.call-start = ((), (), s32[]{:S(2)}) async-start(), calls=%async_computation.22 | async-start | bytes 3538944 | tf_op jit(solution)/shard_map/all_gather | solution.py:86
  993.2 405.8 %reduce-scatter.16.cloned.1.call-start = ((), (), s32[]{:S(2)}) async-start(), calls=%async_computation.33 | async-start | bytes 15728640 | tf_op jit(solution)/shard_map/reduce_scatter | solution.py:262
  1262.5 16.1 copy-start.43
  1278.6 9.4 copy-start.49
  1278.6 9.4 copy-start.50
  1278.6 9.4 copy-start.44
  1301.1 102.3 %copy-start.16 = (bf16[2,256,1536]{2,1,0:T(8,128)(2,1)S(1)}, bf16[2,256,1536]{2,1,0:T(8,128)(2,1)}, u32[]{:S(2)}) copy-start(bf16[2,256,1536]{2,1,0:T(8,128)(2,1)} %param.29) | copy-start | bytes 4718596
  1301.1 350.5 %reduce-scatter.18.cloned.1.call-start = ((), (), s32[]{:S(2)}) async-start(), calls=%async_computation.34 | async-start | bytes 3932160 | tf_op jit(solution)/shard_map/reduce_scatter | solution.py:330
  1399.0 4.7 copy-start.12
  1399.0 7.2 slice-start
  1590.5 78.6 %reduce-scatter.20.cloned.1.call-start = ((), (), s32[]{:S(2)}) async-start(), calls=%async_computation.35 | async-start | bytes 3932160 | tf_op jit(solution)/shard_map/reduce_scatter | solution.py:333
  1591.3 156.0 %reduce-scatter.34.cloned.1.call-start = ((), (), s32[]{:S(2)}) async-start(), calls=%async_computation.42 | async-start | bytes 3538944
  1610.2 214.4 %reduce-scatter.32.cloned.1.call-start = ((), (), s32[]{:S(2)}) async-start(), calls=%async_computation.41 | async-start | bytes 3538944 | tf_op jit(solution)/shard_map/reduce_scatter | solution.py:274
  1621.5 280.5 %reduce-scatter.30.cloned.1.call-start = ((), (), s32[]{:S(2)}) async-start(), calls=%async_computation.40 | async-start | bytes 3538944 | tf_op jit(solution)/shard_map/reduce_scatter | solution.py:271
  1633.0 367.6 %reduce-scatter.28.cloned.1.call-start = ((), (), s32[]{:S(2)}) async-start(), calls=%async_computation.39 | async-start | bytes 5308416 | tf_op jit(solution)/shard_map/reduce_scatter | solution.py:50
  1640.6 459.1 %reduce-scatter.22.cloned.1.call-start = ((), (), s32[]{:S(2)}) async-start(), calls=%async_computation.36 | async-start | bytes 5308416 | tf_op jit(solution)/shard_map/reduce_scatter | solution.py:41
  1640.6 4.7 copy-start.19
  1651.5 520.9 %reduce-scatter.24.cloned.1.call-start = ((), (), s32[]{:S(2)}) async-start(), calls=%async_computation.37 | async-start | bytes 2654208 | tf_op jit(solution)/shard_map/reduce_scatter | solution.py:44
  1656.2 13.0 copy-start.26
  1659.0 585.4 %reduce-scatter.26.cloned.1.call-start = ((), (), s32[]{:S(2)}) async-start(), calls=%async_computation.38 | async-start | bytes 2654208 | tf_op jit(solution)/shard_map/reduce_scatter | solution.py:47
  1673.1 619.8 %all-reduce.14.cloned.1.call-start = ((), (), s32[]{:S(2)}) async-start(), calls=%async_computation.43 | async-start | bytes 3538944 | tf_op jit(solution)/shard_map/psum | solution.py:61
  1903.9 5.3 copy-start.15
  1911.6 332.9 %copy-start.39 = (f32[1,2,2,128]{3,1,2,0:T(2,128)S(1)}, f32[1,2,2,128]{3,1,2,0:T(2,128)}, u32[]{:S(2)}) copy-start(f32[1,2,2,128]{3,1,2,0:T(2,128)} %copy-done.38) | copy-start | bytes 6148
  1911.6 332.9 %copy-start.42 = (bf16[1536]{0:T(1024)(128)(2,1)S(1)}, bf16[1536]{0:T(1024)(128)(2,1)}, u32[]{:S(2)}) copy-start(bf16[1536]{0:T(1024)(128)(2,1)} %get-tuple-element.343) | copy-start | bytes 9220
  2292.9 5.9 copy-start.29
  (27 other events, 64.9 us)
Sparse Core Ops, SparseCore 0:
  10.2 55.0 all-gather.25
  67.5 50.7 all-gather.21
  120.4 78.4 all-gather.29
  200.9 27.0 all-gather.27
  230.0 28.9 all-gather.23
  261.0 79.8 all-gather.31
  343.1 58.5 all-gather.35
  403.8 44.9 all-gather.33
  451.1 60.4 all-gather.37
  513.6 59.0 all-gather.39
  593.0 56.9 reduce-scatter.13
  654.1 52.3 all-gather.45
  708.9 50.6 all-gather.49
  761.8 78.4 all-gather.53
  842.3 27.0 all-gather.47
  871.5 28.9 all-gather.51
  902.7 79.8 all-gather.55
  984.9 58.5 all-gather.61
  1045.2 44.9 all-gather.57
  1092.5 60.4 all-gather.59
  1154.6 45.0 all-gather.43
  1202.1 60.4 all-gather.41
  1301.2 97.6 reduce-scatter.15
  1590.7 37.9 reduce-scatter.17
  1631.2 37.9 reduce-scatter.19
  1673.0 74.2 reduce-scatter.33
  1751.2 73.3 reduce-scatter.31
  1828.6 73.3 reduce-scatter.29
  1906.1 94.4 reduce-scatter.27
  2004.5 95.1 reduce-scatter.21
  2103.6 68.7 reduce-scatter.23
  2176.3 68.0 reduce-scatter.25
  2247.1 45.7 all-reduce.13
where the time goes:
time: 2320 us; the launch traced here: 2310 us
  waiting for transfers between devices  1630 us (70%)
  matrix products  333 us (14%)
  local copies, waits for them, and re-layouts  171 us (7%)
  other arithmetic  81.4 us (4%)
  blocking collectives  75.4 us (3%)
    all_gather x2, waiting for transfers between devices, gather_attention(): lax.all_gather(shard_query, 'fsdp', axis=0, tiled=True)  144 us
    all_gather x2, waiting for transfers between devices, gather_mlp(): lax.all_gather(shard_down, 'fsdp', axis=1, tiled=True)  124 us
    all_gather x2, waiting for transfers between devices, gather_mlp(): lax.all_gather(shard_up, 'fsdp', axis=0, tiled=True)  102 us
    all_gather x2, waiting for transfers between devices, gather_mlp(): lax.all_gather(shard_gate, 'fsdp', axis=0, tiled=True)  101 us
    reduce_scatter x1, waiting for transfers between devices, reduce_grads(): lax.psum_scatter(parts[0].astype(jnp.bfloat16), 'fsdp', scatter_dimension...  99.1 us
    reduce_scatter x1, waiting for transfers between devices, on_device(): lax.psum_scatter(part_normed_two.reshape(seq_count, length, model_width),...  97.8 us
    all_gather x2, waiting for transfers between devices, forward(): lax.all_gather(normed_two.reshape(seq_count, tok_local, model_width), 'co...  93.9 us
    reduce_scatter x1, waiting for transfers between devices, reduce_grads(): lax.psum_scatter(parts[3].astype(jnp.bfloat16), 'fsdp', scatter_dimension...  85.3 us
  transfers between devices with their start and end apart: 33, of which 32 were waited for; matrix products, arithmetic and copies ran while one was open for 14% of the time, Pallas kernels for 0%

commit v1 on v0

--- a/solution.py
+++ b/solution.py
@@ -9,6 +9,28 @@
 HD = 96
 EPSILON = 1e-05
 THETA = 100000.0
+
+
+def laid_out(tiles, dim):
+    tiles = jnp.moveaxis(tiles, 0, dim)
+    shape = tiles.shape
+    return tiles.reshape(*shape[:dim], shape[dim] * shape[dim + 1], *shape[dim + 2 :])
+
+
+def ring_gather(value, axis, dim):
+    devices = lax.axis_size(axis)
+    pairs = [(i, (i + 1) % devices) for i in range(devices)]
+    back = [(b, a) for a, b in pairs]
+    lower, upper = ([], [])
+    for lap in range(devices - 1):
+        if lap % 2 == 0:
+            lower.append(lax.ppermute(lower[-1] if lower else value, axis, pairs))
+        else:
+            upper.append(lax.ppermute(upper[-1] if upper else value, axis, back))
+    blocks = jnp.stack([*lower[::-1], value, *upper])
+    shift = lax.axis_index(axis) - len(lower)
+    blocks = blocks[(jnp.arange(devices) - shift) % devices]
+    return laid_out(blocks, dim)
 
 
 def rms_scale(values, gain):
@@ -72,7 +94,7 @@
     return (
         lax.all_gather(shard_query, "fsdp", axis=0, tiled=True),
         lax.all_gather(shard_key, "fsdp", axis=0, tiled=True),
-        lax.all_gather(shard_value, "fsdp", axis=0, tiled=True),
+        ring_gather(shard_value, "fsdp", 0),
         lax.all_gather(shard_out, "fsdp", axis=0, tiled=True),
         lax.all_gather(shard_gain_a, "fsdp", axis=0, tiled=True),
         lax.all_gather(shard_gain_m, "fsdp", axis=0, tiled=True),

time: 2320 us -> 2250 us (0.970)
  waiting for transfers between devices: 1630 us -> 1520 us
  starting transfers between devices: 2.31 us -> 28 us
    all_gather x2 -> x0, waiting for transfers between devices: 71.6 us -> none  [gather_attention(): lax.all_gather(shard_value, 'fsdp', axis=0, tiled=True)]
    ppermute x0 -> x14, waiting for transfers between devices: none -> 71.1 us  [the longest x8 45.5 us: ring_gather(): lower.append(lax.ppermute(lower[-1] if lower else value, axis, pairs))]
    all_gather x2, waiting for transfers between devices: 63.9 us -> 0.02 us  [gather_attention(): lax.all_gather(shard_key, 'fsdp', axis=0, tiled=True)]
    all_gather x2, waiting for transfers between devices: 144 us -> 105 us  [gather_attention(): lax.all_gather(shard_query, 'fsdp', axis=0, tiled=True)]
    ppermute x0 -> x14, starting transfers between devices: none -> 25.8 us  [the longest x6 18.8 us: ring_gather(): upper.append(lax.ppermute(upper[-1] if upper else value, axis, back))]
    unnamed x34 -> x32, waiting for transfers between devices: 82.6 us -> 81.1 us
  transfers between devices with their start and end apart: 33 -> 45, of which waited for: 32 -> 36; matrix products, arithmetic and copies ran while one was open for 14% -> 15% of each run, Pallas kernels for 0% -> 0%
where the time goes in v1:
time: 2250 us; the launch traced here: 2240 us
  waiting for transfers between devices  1520 us (68%)
  matrix products  333 us (15%)
  local copies, waits for them, and re-layouts  180 us (8%)
  other arithmetic  82.3 us (4%)
  blocking collectives  75.5 us (3%)
  starting transfers between devices  28 us (1%)
    all_gather x2, waiting for transfers between devices, gather_mlp(): lax.all_gather(shard_down, 'fsdp', axis=1, tiled=True)  124 us
    all_gather x2, waiting for transfers between devices, gather_attention(): lax.all_gather(shard_query, 'fsdp', axis=0, tiled=True)  105 us
    all_gather x2, waiting for transfers between devices, gather_mlp(): lax.all_gather(shard_up, 'fsdp', axis=0, tiled=True)  102 us
    all_gather x2, waiting for transfers between devices, gather_mlp(): lax.all_gather(shard_gate, 'fsdp', axis=0, tiled=True)  101 us
    reduce_scatter x1, waiting for transfers between devices, reduce_grads(): lax.psum_scatter(parts[0].astype(jnp.bfloat16), 'fsdp', scatter_dimension...  99.1 us
    reduce_scatter x1, waiting for transfers between devices, on_device(): lax.psum_scatter(part_normed_two.reshape(seq_count, length, model_width),...  97.8 us
    all_gather x2, waiting for transfers between devices, forward(): lax.all_gather(normed_two.reshape(seq_count, tok_local, model_width), 'co...  93.7 us
    reduce_scatter x1, waiting for transfers between devices, reduce_grads(): lax.psum_scatter(parts[3].astype(jnp.bfloat16), 'fsdp', scatter_dimension...  85.2 us
  transfers between devices with their start and end apart: 45, of which 36 were waited for; matrix products, arithmetic and copies ran while one was open for 15% of the time, Pallas kernels for 0%

profile of v1, /device:TPU:0, one launch (start us, length us, event | category | flops | bytes accessed | tf_op | source)
XLA Modules:
  0.0 2237.7 jit_solution(1122833712052298900)
XLA Ops:
  11.7 10.3 collective-permute-done
  26.7 12.6 collective-permute-done.1
  45.2 22.2 all-reduce.9
  71.6 9.5 collective-permute-done.5
  114.1 49.4 %all-gather.26.cloned.1.call-done = bf16[1536,1536]{1,0:T(8,128)(2,1)} async-done(((bf16[192,1536]{1,0:T(8,128)(2,1)}), bf16[1536,1536]{1,0:T(8,128)(2,1)}) %all-gather.26.cloned.1.call-update) | async-done | bytes 4718608 | tf_op jit(solution)/shard_map/all_gather | solution.py:95
  177.5 15.2 all-gather.20.cloned.1.call-done
  192.7 30.9 %all-gather.24.cloned.1.call-done = bf16[2,1024,768]{1,2,0:T(8,128)(2,1)} async-done(((bf16[2,256,768]{1,2,0:T(8,128)(2,1)}), bf16[2,1024,768]{1,2,0:T(8,128)(2,1)}) %all-gather.24.cloned.1.call-update) | async-done | bytes 3145744 | tf_op jit(solution)/shard_map/all_gather | solution.py:199
  225.0 43.3 %while.39 = (s32[]{:T(128)}, bf16[2,256,8,2,96]{1,4,3,2,0:T(8,128)(2,1)}, bf16[2,1024,768]{1,2,0:T(8,128)(2,1)}, s32[2,256]{1,0:T(2,128)S(1)}, s32[2,1024]{1,0:T...) while((s32[]{:T(128)}, ...), condition=%wide.region_6.7_spmd.clone, body=%wide.region_3.6_spmd.clone.sunk | while | flops 1636959488 | bytes 45139068 | solution.py:207
  227.5 10.7 fusion.222
  248.9 10.7 fusion.222
  259.6 8.7 fusion.223
  271.8 33.8 %all-gather.28.cloned.1.call-done = bf16[1536,1536]{1,0:T(8,128)(2,1)} async-done(((bf16[192,1536]{1,0:T(8,128)(2,1)}), bf16[1536,1536]{1,0:T(8,128)(2,1)}) %all-gather.28.cloned.1.call-update) | async-done | bytes 4718608 | tf_op jit(solution)/shard_map/all_gather | solution.py:98
  315.7 50.6 %all-gather.32.cloned.1.call-done = bf16[1536,1024]{1,0:T(8,128)(2,1)} async-done(((bf16[192,1024]{1,0:T(8,128)(2,1)}), bf16[1536,1024]{1,0:T(8,128)(2,1)}) %all-gather.32.cloned.1.call-update) | async-done | bytes 3145744 | tf_op jit(solution)/shard_map/all_gather | solution.py:106
  366.3 47.2 %all-gather.30.cloned.1.call-done = bf16[2,1024,1536]{2,1,0:T(8,128)(2,1)} async-done(((bf16[2,256,1536]{2,1,0:T(8,128)(2,1)}), bf16[2,1024,1536]{2,1,0:T(8,128)(2,1)}) %all-gather.30.cloned.1.call-update) | async-done | bytes 6291472 | tf_op jit(solution)/shard_map/all_gather | solution.py:212
  413.5 11.7 fusion.116
  425.2 51.0 %all-gather.34.cloned.1.call-done = bf16[1536,1024]{1,0:T(8,128)(2,1)} async-done(((bf16[192,1024]{1,0:T(8,128)(2,1)}), bf16[1536,1024]{1,0:T(8,128)(2,1)}) %all-gather.34.cloned.1.call-update) | async-done | bytes 3145744 | tf_op jit(solution)/shard_map/all_gather | solution.py:107
  476.1 61.3 %all-gather.36.cloned.1.call-done = bf16[1024,1536]{0,1:T(8,128)(2,1)} async-done(((bf16[1024,192]{0,1:T(8,128)(2,1)}), bf16[1024,1536]{0,1:T(8,128)(2,1)}) %all-gather.36.cloned.1.call-update) | async-done | bytes 3145744 | tf_op jit(solution)/shard_map/all_gather | solution.py:108
  537.4 20.2 convolution_convert_fusion.2
  557.7 57.0 %reduce-scatter.14.cloned.1.call-done = bf16[2,256,1536]{2,1,0:T(8,128)(2,1)} async-done(((bf16[2,1024,1536]{2,1,0:T(8,128)(2,1)}), bf16[2,256,1536]{2,1,0:T(8,128)(2,1)}) %reduce-scatter.14.cloned.1.call-update) | async-done | bytes 1572880 | tf_op jit(solution)/shard_map/reduce_scatter | solution.py:220
  620.9 10.1 collective-permute-done.7
  635.7 12.6 collective-permute-done.8
  648.8 23.0 %all-reduce.8 = (bf16[1536]{0:T(1024)(128)(2,1)S(1)}, bf16[1536]{0:T(1024)(128)(2,1)S(1)}) all-reduce(bf16[1536]{0:T(1024)(128)(2,1)S(1)} %dynamic-update-slice.2, bf16[1536]{0:T(1024)(128)(2,1)S(1)} %dynamic-update-slice.3), channel_id=1, replica_groups=mesh['fsdp'=8,'context'=4] {'fsdp'}, use_global_device_ids=true, to_apply=%add.3 | all-reduce | flops 3072 | bytes 12288
  677.3 10.3 collective-permute-done.12
  714.9 55.8 %all-gather.48.cloned.1.call-done = bf16[1536,1536]{1,0:T(8,128)(2,1)} async-done(((bf16[192,1536]{1,0:T(8,128)(2,1)}), bf16[1536,1536]{1,0:T(8,128)(2,1)}) %all-gather.48.cloned.1.call-update) | async-done | bytes 4718608 | tf_op jit(solution)/shard_map/all_gather | solution.py:95
  783.4 16.7 all-gather.42.cloned.1.call-done
  800.1 31.0 %all-gather.46.cloned.1.call-done = bf16[2,1024,768]{1,2,0:T(8,128)(2,1)} async-done(((bf16[2,256,768]{1,2,0:T(8,128)(2,1)}), bf16[2,1024,768]{1,2,0:T(8,128)(2,1)}) %all-gather.46.cloned.1.call-update) | async-done | bytes 3145744 | tf_op jit(solution)/shard_map/all_gather | solution.py:199
  832.4 57.1 %while.40 = (s32[]{:T(128)}, bf16[2,256,8,2,96]{1,4,3,2,0:T(8,128)(2,1)}, f32[2,8,2,256,1]{3,2,1,4,0:T(2,128)S(1)}, bf16[2,1024,768]{1,2,0:T(8,128)(2,1)}, s32[2...) while((s32[]{:T(128)}, ...), condition=%wide.region_12.13_spmd.clone, body=%wide.region_9.12_spmd.clone.sunk | while | flops 1662120192 | bytes 62538888 | solution.py:207
  842.5 9.2 fusion.228
  851.7 9.1 fusion.229
  871.0 9.2 fusion.228
  880.2 9.1 fusion.229
  894.2 19.0 all-gather.50.cloned.1.call-done
  923.7 50.5 %all-gather.56.cloned.1.call-done = bf16[1536,1024]{1,0:T(8,128)(2,1)} async-done(((bf16[192,1024]{1,0:T(8,128)(2,1)}), bf16[1536,1024]{1,0:T(8,128)(2,1)}) %all-gather.56.cloned.1.call-update) | async-done | bytes 3145744 | tf_op jit(solution)/shard_map/all_gather | solution.py:106
  974.2 46.5 %all-gather.52.cloned.1.call-done = bf16[2,1024,1536]{2,1,0:T(8,128)(2,1)} async-done(((bf16[2,256,1536]{2,1,0:T(8,128)(2,1)}), bf16[2,1024,1536]{2,1,0:T(8,128)(2,1)}) %all-gather.52.cloned.1.call-update) | async-done | bytes 6291472 | tf_op jit(solution)/shard_map/all_gather | solution.py:212
  1020.7 11.7 fusion.120
  1032.4 51.0 %all-gather.54.cloned.1.call-done = bf16[1536,1024]{1,0:T(8,128)(2,1)} async-done(((bf16[192,1024]{1,0:T(8,128)(2,1)}), bf16[1536,1024]{1,0:T(8,128)(2,1)}) %all-gather.54.cloned.1.call-update) | async-done | bytes 3145744 | tf_op jit(solution)/shard_map/all_gather | solution.py:107
  1083.4 11.7 fusion.119
  1095.1 35.0 %all-gather.40.cloned.1.call-done = bf16[2,1024,1536]{2,1,0:T(8,128)(2,1)} async-done(((bf16[2,256,1536]{2,1,0:T(8,128)(2,1)}), bf16[2,1024,1536]{2,1,0:T(8,128)(2,1)}) %all-gather.40.cloned.1.call-update) | async-done | bytes 6291472 | tf_op jit(solution)/shard_map/all_gather | solution.py:272
  1130.1 62.7 %all-gather.38.cloned.1.call-done = bf16[1024,1536]{0,1:T(8,128)(2,1)} async-done(((bf16[1024,192]{0,1:T(8,128)(2,1)}), bf16[1024,1536]{0,1:T(8,128)(2,1)}) %all-gather.38.cloned.1.call-update) | async-done | bytes 3145744 | tf_op jit(solution)/shard_map/all_gather | solution.py:108
  1192.9 16.1 fusion.78
  1209.0 9.5 fusion.121
  1218.5 13.1 convolution_add_fusion
  1231.6 97.8 %reduce-scatter.16.cloned.1.call-done = f32[2,256,1536]{2,1,0:T(8,128)} async-done(((f32[2,1024,1536]{2,1,0:T(8,128)}), f32[2,256,1536]{2,1,0:T(8,128)}) %reduce-scatter.16.cloned.1.call-update) | async-done | bytes 3145744 | tf_op jit(solution)/shard_map/reduce_scatter | solution.py:284
  1348.0 172.9 %while.41 = (s32[]{:T(128)}, f32[2,256,8,2,96]{1,0,4,3,2:T(2,128)}, bf16[2,1024,768]{1,2,0:T(8,128)(2,1)}, bf16[2,1024,768]{2,1,0:T(8,128)(2,1)}, bf16[2,1024,76...) while((s32[]{:T(128)}, f32[2,256,8,2,96]{1,0,4,3,2:T(2,128)}, ...), condition=%wide.region_18.19_spmd.clone, body=%wide.region_16.18_spmd.clone.sunk | while | flops 4067029248 | bytes 192513344 | solution.py:348
  1354.6 10.7 fusion.241
  1365.3 9.9 fusion.242
  1398.2 32.3 %dynamic_update_slice.44 = f32[2,256,8,2,96]{1,0,4,3,2:T(2,128)} dynamic-update-slice(f32[2,256,8,2,96]{1,0,4,3,2:T(2,128)} %get-tuple-element.728, f32[1,256,8,2,96]{1,0,4,3,2:T(1,128)S(1)} %copy.145, s32[]{:T(128)S(6)} %copy.191, s32[]{:T(128)} %constant.125.clone.1..sunk, s32[]{:T(128)} %constant.125.clone.1..sunk, s32[]{:T(128)} %constant.125.clone.1..sunk, s32[]{:T(128)} %constant.125.clone.1..sunk) | dynamic-update-slice | bytes 3145732 | tf_op jit(solution)/shard_map/while/body/jit(dynamic_update_index_in_dim)/dynamic_update_slice | solution.py:348
  1440.9 10.7 fusion.241
  1451.6 9.9 fusion.242
  1461.4 8.7 fusion.243
  1484.5 32.3 %dynamic_update_slice.44 = f32[2,256,8,2,96]{1,0,4,3,2:T(2,128)} dynamic-update-slice(f32[2,256,8,2,96]{1,0,4,3,2:T(2,128)} %get-tuple-element.728, f32[1,256,8,2,96]{1,0,4,3,2:T(1,128)S(1)} %copy.145, s32[]{:T(128)S(6)} %copy.191, s32[]{:T(128)} %constant.125.clone.1..sunk, s32[]{:T(128)} %constant.125.clone.1..sunk, s32[]{:T(128)} %constant.125.clone.1..sunk, s32[]{:T(128)} %constant.125.clone.1..sunk) | dynamic-update-slice | bytes 3145732 | tf_op jit(solution)/shard_map/while/body/jit(dynamic_update_index_in_dim)/dynamic_update_slice | solution.py:348
  1521.7 15.8 fusion.82
  1540.5 11.3 convolution_convert_fusion.3
  1551.9 11.3 convolution_convert_fusion.4
  1589.5 10.1 reduce-scatter.20.cloned.1.call-done
  1604.3 73.5 %reduce-scatter.34.cloned.1.call-done = bf16[192,1024]{1,0:T(8,128)(2,1)} async-done(((bf16[1536,1024]{1,0:T(8,128)(2,1)}), bf16[192,1024]{1,0:T(8,128)(2,1)}) %reduce-scatter.34.cloned.1.call-update) | async-done | bytes 393232
  1680.3 75.3 %reduce-scatter.32.cloned.1.call-done = bf16[192,1024]{1,0:T(8,128)(2,1)} async-done(((bf16[1536,1024]{1,0:T(8,128)(2,1)}), bf16[192,1024]{1,0:T(8,128)(2,1)}) %reduce-scatter.32.cloned.1.call-update) | async-done | bytes 393232 | tf_op jit(solution)/shard_map/reduce_scatter | solution.py:296
  1757.6 75.3 %reduce-scatter.30.cloned.1.call-done = bf16[192,1024]{1,0:T(8,128)(2,1)} async-done(((bf16[1536,1024]{1,0:T(8,128)(2,1)}), bf16[192,1024]{1,0:T(8,128)(2,1)}) %reduce-scatter.30.cloned.1.call-update) | async-done | bytes 393232 | tf_op jit(solution)/shard_map/reduce_scatter | solution.py:293
  1846.1 85.2 %reduce-scatter.28.cloned.1.call-done = bf16[192,1536]{1,0:T(8,128)(2,1)} async-done(((bf16[1536,1536]{1,0:T(8,128)(2,1)}), bf16[192,1536]{1,0:T(8,128)(2,1)}) %reduce-scatter.28.cloned.1.call-update) | async-done | bytes 589840 | tf_op jit(solution)/shard_map/reduce_scatter | solution.py:72
  1931.3 99.1 %reduce-scatter.22.cloned.1.call-done = bf16[192,1536]{1,0:T(8,128)(2,1)} async-done(((bf16[1536,1536]{1,0:T(8,128)(2,1)}), bf16[192,1536]{1,0:T(8,128)(2,1)}) %reduce-scatter.22.cloned.1.call-update) | async-done | bytes 589840 | tf_op jit(solution)/shard_map/reduce_scatter | solution.py:63
  2030.4 72.7 %reduce-scatter.24.cloned.1.call-done = bf16[192,768]{1,0:T(8,128)(2,1)} async-done(((bf16[1536,768]{1,0:T(8,128)(2,1)}), bf16[192,768]{1,0:T(8,128)(2,1)}) %reduce-scatter.24.cloned.1.call-update) | async-done | bytes 294928 | tf_op jit(solution)/shard_map/reduce_scatter | solution.py:66
  2103.1 71.9 %reduce-scatter.26.cloned.1.call-done = bf16[192,768]{1,0:T(8,128)(2,1)} async-done(((bf16[1536,768]{1,0:T(8,128)(2,1)}), bf16[192,768]{1,0:T(8,128)(2,1)}) %reduce-scatter.26.cloned.1.call-update) | async-done | bytes 294928 | tf_op jit(solution)/shard_map/reduce_scatter | solution.py:69
  2175.0 19.5 all-reduce.7
  2206.7 16.9 all-reduce.14.cloned.1.call-done
  (397 shorter events, 333.8 us)
Async XLA Ops:
  7.2 62.8 %copy-start.7 = (bf16[2,256,1536]{2,1,0:T(8,128)(2,1)S(1)}, bf16[2,256,1536]{2,1,0:T(8,128)(2,1)}, u32[]{:S(2)}) copy-start(bf16[2,256,1536]{2,1,0:T(8,128)(2,1)} %param.18) | copy-start | bytes 4718596
  7.2 95.8 %all-gather.22.cloned.1.call-start = ((), (), s32[]{:S(2)}) async-start(), calls=%async_computation.12 | async-start | bytes 2654208 | tf_op jit(solution)/shard_map/all_gather | solution.py:96
  7.9 155.6 %all-gather.26.cloned.1.call-start = ((), (), s32[]{:S(2)}) async-start(), calls=%async_computation.14 | async-start | bytes 5308416 | tf_op jit(solution)/shard_map/all_gather | solution.py:95
  8.7 184.0 %all-gather.20.cloned.1.call-start = ((), (), s32[]{:S(2)}) async-start(), calls=%async_computation.11 | async-start | bytes 3932160 | tf_op jit(solution)/shard_map/all_gather | solution.py:200
  8.7 13.2 collective-permute-start
  22.0 17.3 collective-permute-start.1
  22.0 46.0 %collective-permute-start.4 = (bf16[192,768]{1,0:T(8,128)(2,1)}, bf16[192,768]{1,0:T(8,128)(2,1)S(1)}, u32[]{:S(2)}, u32[]{:S(2)}) collective-permute-start(bf16[192,768]{1,0:T(8,128)(2,1)} %param.22), channel_id=1, source_target_pairs={{4,0},{8,4},{12,8},{16,12},{20,16},{24,20},{28,24},{0,28},{5,1},{9... | collective-permute-start | bytes 884744 | tf_op jit(solution)/shard_map/ppermute | solution.py:29
  39.3 28.7 %collective-permute-start.2 = (bf16[192,768]{1,0:T(8,128)(2,1)S(1)}, bf16[192,768]{1,0:T(8,128)(2,1)S(1)}, u32[]{:S(2)}, u32[]{:S(2)}) collective-permute-start(bf16[192,768]{1,0:T(8,128)(2,1)S(1)} %collective-permute-done.1), channel_id=1, source_target_pairs={{0,4},{4,8},{8,12},{12,16},{16,20},{20,24},{24,28},{28,0},{1,5},{5... | collective-permute-start | bytes 884744 | tf_op jit(solution)/shard_map/ppermute | solution.py:27
  41.5 41.9 %copy-start.29 = (bf16[192,768]{1,0:T(8,128)(2,1)S(1)}, bf16[192,768]{1,0:T(8,128)(2,1)}, u32[]{:S(2)}) copy-start(bf16[192,768]{1,0:T(8,128)(2,1)} %param.22) | copy-start | bytes 884740
  68.0 13.4 copy-start.41
  68.0 13.2 collective-permute-start.5
  68.0 13.4 collective-permute-start.3
  71.6 18.6 copy-start.45
  81.2 6.9 collective-permute-start.6
  95.2 128.4 %all-gather.24.cloned.1.call-start = ((), (), s32[]{:S(2)}) async-start(), calls=%async_computation.13 | async-start | bytes 3932160 | tf_op jit(solution)/shard_map/all_gather | solution.py:199
  103.0 71.9 %copy-start.17 = (f32[512,48]{0,1:T(8,128)}, f32[512,48]{0,1:T(8,128)S(1)}, u32[]{:S(2)}) copy-start(f32[512,48]{0,1:T(8,128)S(1)} %get-tuple-element.445) | copy-start | bytes 294916
  103.0 72.0 %copy-start.20 = (f32[512,48]{0,1:T(8,128)}, f32[512,48]{0,1:T(8,128)S(1)}, u32[]{:S(2)}) copy-start(f32[512,48]{0,1:T(8,128)S(1)} %get-tuple-element.444) | copy-start | bytes 294916
  112.0 193.7 %all-gather.28.cloned.1.call-start = ((), (), s32[]{:S(2)}) async-start(), calls=%async_computation.15 | async-start | bytes 5308416 | tf_op jit(solution)/shard_map/all_gather | solution.py:98
  112.5 253.7 %all-gather.32.cloned.1.call-start = ((), (), s32[]{:S(2)}) async-start(), calls=%async_computation.17 | async-start | bytes 3538944 | tf_op jit(solution)/shard_map/all_gather | solution.py:106
  113.1 300.3 %all-gather.30.cloned.1.call-start = ((), (), s32[]{:S(2)}) async-start(), calls=%async_computation.16 | async-start | bytes 7864320 | tf_op jit(solution)/shard_map/all_gather | solution.py:212
  268.3 37.4 %copy-start.8 = (bf16[2,256,1536]{2,1,0:T(8,128)(2,1)S(1)}, bf16[2,256,1536]{2,1,0:T(8,128)(2,1)}, u32[]{:S(2)}) copy-start(bf16[2,256,1536]{2,1,0:T(8,128)(2,1)} %param.18) | copy-start | bytes 4718596
  313.6 162.5 %all-gather.34.cloned.1.call-start = ((), (), s32[]{:S(2)}) async-start(), calls=%async_computation.18 | async-start | bytes 3538944 | tf_op jit(solution)/shard_map/all_gather | solution.py:107
  314.4 223.1 %all-gather.36.cloned.1.call-start = ((), (), s32[]{:S(2)}) async-start(), calls=%async_computation.19 | async-start | bytes 3538944 | tf_op jit(solution)/shard_map/all_gather | solution.py:108
  315.1 299.6 %reduce-scatter.14.cloned.1.call-start = ((), (), s32[]{:S(2)}) async-start(), calls=%async_computation.20 | async-start | bytes 7864320 | tf_op jit(solution)/shard_map/reduce_scatter | solution.py:220
  557.6 61.7 %copy-start.30 = (bf16[192,768]{1,0:T(8,128)(2,1)S(1)}, bf16[192,768]{1,0:T(8,128)(2,1)}, u32[]{:S(2)}) copy-start(bf16[192,768]{1,0:T(8,128)(2,1)} %param.22) | copy-start | bytes 884740
  557.6 90.7 %copy-start.49 = (bf16[192]{0:T(256)(128)(2,1)S(1)}, bf16[192]{0:T(256)(128)(2,1)}, u32[]{:S(2)}) copy-start(bf16[192]{0:T(256)(128)(2,1)} %param.28) | copy-start | bytes 1156
  557.6 90.9 %copy-start.50 = (bf16[192]{0:T(256)(128)(2,1)S(1)}, bf16[192]{0:T(256)(128)(2,1)}, u32[]{:S(2)}) copy-start(bf16[192]{0:T(256)(128)(2,1)} %param.27) | copy-start | bytes 1156
  557.6 118.1 %copy-start.42 = (f32[2,256]{1,0:T(2,128)S(1)}, f32[2,256]{1,0:T(2,128)}, u32[]{:S(2)}) copy-start(f32[2,256]{1,0:T(2,128)} %copy-done.41) | copy-start | bytes 6148
  557.7 146.8 %all-gather.44.cloned.1.call-start = ((), (), s32[]{:S(2)}) async-start(), calls=%async_computation.24 | async-start | bytes 2654208 | tf_op jit(solution)/shard_map/all_gather | solution.py:96
  618.7 152.0 %all-gather.48.cloned.1.call-start = ((), (), s32[]{:S(2)}) async-start(), calls=%async_computation.26 | async-start | bytes 5308416 | tf_op jit(solution)/shard_map/all_gather | solution.py:95
  619.3 180.8 %all-gather.42.cloned.1.call-start = ((), (), s32[]{:S(2)}) async-start(), calls=%async_computation.23 | async-start | bytes 3932160 | tf_op jit(solution)/shard_map/all_gather | solution.py:200
  619.4 11.6 collective-permute-start.7
  631.0 17.3 collective-permute-start.8
  631.0 40.8 %collective-permute-start.11 = (bf16[192,768]{1,0:T(8,128)(2,1)S(1)}, bf16[192,768]{1,0:T(8,128)(2,1)S(1)}, u32[]{:S(2)}, u32[]{:S(2)}) collective-permute-start(bf16[192,768]{1,0:T(8,128)(2,1)S(1)} %copy-done.30), channel_id=1, source_target_pairs={{4,0},{8,4},{12,8},{16,12},{20,16},{24,20},{28,24},{0,28},{5,1},{9... | collective-permute-start | bytes 884744 | tf_op jit(solution)/shard_map/ppermute | solution.py:29
  648.3 44.6 %copy-start.34 = (bf16[192,768]{1,0:T(8,128)(2,1)}, bf16[192,768]{1,0:T(8,128)(2,1)S(1)}, u32[]{:S(2)}) copy-start(bf16[192,768]{1,0:T(8,128)(2,1)S(1)} %collective-permute-done.8) | copy-start | bytes 884740
  648.3 27.5 %collective-permute-start.9 = (bf16[192,768]{1,0:T(8,128)(2,1)S(1)}, bf16[192,768]{1,0:T(8,128)(2,1)S(1)}, u32[]{:S(2)}, u32[]{:S(2)}) collective-permute-start(bf16[192,768]{1,0:T(8,128)(2,1)S(1)} %collective-permute-done.8), channel_id=1, source_target_pairs={{0,4},{4,8},{8,12},{12,16},{16,20},{20,24},{24,28},{28,0},{1,5},{5... | collective-permute-start | bytes 884744 | tf_op jit(solution)/shard_map/ppermute | solution.py:27
  671.8 23.1 %copy-start.38 = (f32[1536]{0:T(1024)}, f32[1536]{0:T(1024)S(1)}, u32[]{:S(2)}) copy-start(f32[1536]{0:T(1024)S(1)} %convert_element_type.263) | copy-start | bytes 18436
  671.8 15.8 collective-permute-start.12
  675.7 17.1 copy-start.35
  675.7 17.1 collective-permute-start.10
  687.7 9.4 collective-permute-start.13
  704.3 126.8 %all-gather.46.cloned.1.call-start = ((), (), s32[]{:S(2)}) async-start(), calls=%async_computation.25 | async-start | bytes 3932160 | tf_op jit(solution)/shard_map/all_gather | solution.py:199
  713.6 199.7 %all-gather.50.cloned.1.call-start = ((), (), s32[]{:S(2)}) async-start(), calls=%async_computation.27 | async-start | bytes 5308416 | tf_op jit(solution)/shard_map/all_gather | solution.py:98
  714.2 260.0 %all-gather.56.cloned.1.call-start = ((), (), s32[]{:S(2)}) async-start(), calls=%async_computation.30 | async-start | bytes 3538944 | tf_op jit(solution)/shard_map/all_gather | solution.py:106
  714.9 305.8 %all-gather.52.cloned.1.call-start = ((), (), s32[]{:S(2)}) async-start(), calls=%async_computation.28 | async-start | bytes 7864320 | tf_op jit(solution)/shard_map/all_gather | solution.py:212
  889.5 23.7 %copy-start.9 = (bf16[2,256,1536]{2,1,0:T(8,128)(2,1)S(1)}, bf16[2,256,1536]{2,1,0:T(8,128)(2,1)}, u32[]{:S(2)}) copy-start(bf16[2,256,1536]{2,1,0:T(8,128)(2,1)} %param.18) | copy-start | bytes 4718596
  921.7 161.7 %all-gather.54.cloned.1.call-start = ((), (), s32[]{:S(2)}) async-start(), calls=%async_computation.29 | async-start | bytes 3538944 | tf_op jit(solution)/shard_map/all_gather | solution.py:107
  922.3 207.8 %all-gather.40.cloned.1.call-start = ((), (), s32[]{:S(2)}) async-start(), calls=%async_computation.22 | async-start | bytes 7864320 | tf_op jit(solution)/shard_map/all_gather | solution.py:272
  923.0 269.8 %all-gather.38.cloned.1.call-start = ((), (), s32[]{:S(2)}) async-start(), calls=%async_computation.21 | async-start | bytes 3538944 | tf_op jit(solution)/shard_map/all_gather | solution.py:108
  923.6 405.8 %reduce-scatter.16.cloned.1.call-start = ((), (), s32[]{:S(2)}) async-start(), calls=%async_computation.31 | async-start | bytes 15728640 | tf_op jit(solution)/shard_map/reduce_scatter | solution.py:284
  1192.9 16.1 copy-start.46
  1231.5 102.3 %copy-start.16 = (bf16[2,256,1536]{2,1,0:T(8,128)(2,1)S(1)}, bf16[2,256,1536]{2,1,0:T(8,128)(2,1)}, u32[]{:S(2)}) copy-start(bf16[2,256,1536]{2,1,0:T(8,128)(2,1)} %param.29) | copy-start | bytes 4718596
  1231.6 350.4 %reduce-scatter.18.cloned.1.call-start = ((), (), s32[]{:S(2)}) async-start(), calls=%async_computation.32 | async-start | bytes 3932160 | tf_op jit(solution)/shard_map/reduce_scatter | solution.py:352
  1520.9 78.6 %reduce-scatter.20.cloned.1.call-start = ((), (), s32[]{:S(2)}) async-start(), calls=%async_computation.33 | async-start | bytes 3932160 | tf_op jit(solution)/shard_map/reduce_scatter | solution.py:355
  1521.7 156.2 %reduce-scatter.34.cloned.1.call-start = ((), (), s32[]{:S(2)}) async-start(), calls=%async_computation.40 | async-start | bytes 3538944
  1540.5 215.1 %reduce-scatter.32.cloned.1.call-start = ((), (), s32[]{:S(2)}) async-start(), calls=%async_computation.39 | async-start | bytes 3538944 | tf_op jit(solution)/shard_map/reduce_scatter | solution.py:296
  1551.8 281.1 %reduce-scatter.30.cloned.1.call-start = ((), (), s32[]{:S(2)}) async-start(), calls=%async_computation.38 | async-start | bytes 3538944 | tf_op jit(solution)/shard_map/reduce_scatter | solution.py:293
  1563.2 368.1 %reduce-scatter.28.cloned.1.call-start = ((), (), s32[]{:S(2)}) async-start(), calls=%async_computation.37 | async-start | bytes 5308416 | tf_op jit(solution)/shard_map/reduce_scatter | solution.py:72
  1570.8 459.5 %reduce-scatter.22.cloned.1.call-start = ((), (), s32[]{:S(2)}) async-start(), calls=%async_computation.34 | async-start | bytes 5308416 | tf_op jit(solution)/shard_map/reduce_scatter | solution.py:63
  1581.9 521.2 %reduce-scatter.24.cloned.1.call-start = ((), (), s32[]{:S(2)}) async-start(), calls=%async_computation.35 | async-start | bytes 2654208 | tf_op jit(solution)/shard_map/reduce_scatter | solution.py:66
  1589.4 14.2 copy-start.44
  1589.4 585.5 %reduce-scatter.26.cloned.1.call-start = ((), (), s32[]{:S(2)}) async-start(), calls=%async_computation.36 | async-start | bytes 2654208 | tf_op jit(solution)/shard_map/reduce_scatter | solution.py:69
  1603.6 620.0 %all-reduce.14.cloned.1.call-start = ((), (), s32[]{:S(2)}) async-start(), calls=%async_computation.41 | async-start | bytes 3538944 | tf_op jit(solution)/shard_map/psum | solution.py:83
  1842.5 332.5 %copy-start.43 = (bf16[1536]{0:T(1024)(128)(2,1)S(1)}, bf16[1536]{0:T(1024)(128)(2,1)}, u32[]{:S(2)}) copy-start(bf16[1536]{0:T(1024)(128)(2,1)} %get-tuple-element.343) | copy-start | bytes 9220
  (41 other events, 182.0 us)
Sparse Core Ops, SparseCore 0:
  10.2 69.5 all-gather.21
  81.9 81.4 all-gather.25
  165.6 27.0 all-gather.19
  194.7 28.9 all-gather.23
  225.7 79.8 all-gather.27
  307.7 58.5 all-gather.31
  368.4 44.9 all-gather.29
  415.6 60.4 all-gather.33
  478.3 59.0 all-gather.35
  557.7 56.9 reduce-scatter.13
  618.8 69.0 all-gather.43
  690.2 80.4 all-gather.47
  772.9 27.0 all-gather.41
  802.1 28.9 all-gather.45
  833.3 79.8 all-gather.49
  915.5 58.5 all-gather.55
  975.6 44.9 all-gather.51
  1023.0 60.4 all-gather.53
  1085.1 45.0 all-gather.39
  1132.4 60.4 all-gather.37
  1231.7 97.6 reduce-scatter.15
  1521.0 37.9 reduce-scatter.17
  1561.6 37.9 reduce-scatter.19
  1603.4 74.3 reduce-scatter.33
  1681.8 73.7 reduce-scatter.31
  1759.5 73.3 reduce-scatter.29
  1836.9 94.3 reduce-scatter.27
  1935.4 94.9 reduce-scatter.21
  2034.3 68.7 reduce-scatter.23
  2106.8 68.0 reduce-scatter.25
  2177.7 45.7 all-reduce.13
